TPU v7x, 32 devices: a whole 2x2x4 slice. The times are simulated.
32 devices in a mesh: batch: 8 (over z, x), seq: 4 (over y, core).
Axes of the slice: x: 2, y: 2, z: 4, core: 2. Of those that a mesh axis runs over, the one named last changes fastest.
Arguments:
- tokens: bfloat16 [8, 1024, 1024], P('batch', 'seq'), may hold values from -6 to 6
- cotangent: bfloat16 [8, 1024, 1024], P('batch', 'seq'), may hold values from -6 to 6
- image_tokens: bfloat16 [8, 1025, 768], P('batch'), may hold values from -6 to 6
- image_lengths: int32 [8], P('batch'), may hold values from 512 to 1025, as said below
- key_mask: int32 [8, 1025], P('batch'), may hold values 0 or 1
- camera: bfloat16 [8, 1024], P(None, 'batch'), may hold values from -6 to 6
- modulation: bfloat16 [1024, 6144], P('batch'), may hold values from -0.1875 to 0.1875
- q_cross: bfloat16 [1024, 1024], P('batch'), may hold values from -0.1875 to 0.1875
- kv_image: bfloat16 [768, 2048], P('batch'), may hold values from -0.21875 to 0.21875
- out_cross: bfloat16 [1024, 1024], P('batch'), may hold values from -3.5 to 3.5
- qkv_self: bfloat16 [1024, 3072], P('batch'), may hold values from -0.1875 to 0.1875
- out_self: bfloat16 [1024, 1024], P('batch'), may hold values from -6 to 6
- mlp_in: bfloat16 [1024, 4096], P('batch'), may hold values from -0.1875 to 0.1875
- mlp_out: bfloat16 [4096, 1024], P('batch'), may hold values from -0.09375 to 0.09375
Outputs:
- output: bfloat16 [8, 1024, 1024], P('batch', 'seq')
- grad_tokens: float32 [8, 1024, 1024], P('batch', 'seq')
- grad_modulation: float32 [1024, 6144], P('batch')
- grad_q_cross: float32 [1024, 1024], P('batch')
- grad_kv_image: float32 [768, 2048], P('batch')
- grad_out_cross: float32 [1024, 1024], P('batch')
- grad_qkv_self: float32 [1024, 3072], P('batch')
- grad_out_self: float32 [1024, 1024], P('batch')
- grad_mlp_in: float32 [1024, 4096], P('batch')
- grad_mlp_out: float32 [4096, 1024], P('batch')
Inputs may be any that keep to these rules, and one draw needn't show every extreme that they name: `image_lengths`: some object has 1025 valid image tokens and some has 512.
All inputs are finite; a program needn't handle non-finite values. No bound on the sum of `key_mask` on one device may be relied on, other than what follows from the above.
Results may differ from a plain program's by a relative error of at most 0.025.
The roundings to bfloat16 on the way count: a program that leaves them out, or rounds other values in their place, can miss the bound.
Values may be sent and summed in bfloat16 or wider, within the bound.
A program may use at most 256 MiB of HBM per device.

v0:
```python
import functools

import jax
import jax.numpy as jnp
from jax import lax
from jax.experimental import pallas as pl
from jax.experimental.pallas import tpu as pltpu
from jax.sharding import PartitionSpec as P

HEADS = 16
HEAD_DIM = 64


epsilon = 1e-06
group_heads = 4
highest = lax.Precision.HIGHEST
LIMIT = 64 * 1024 * 1024 - 64 * 1024


def modulated_norm(values, shift, scale):
    center = values - jnp.mean(values, axis=-1, keepdims=True)
    normed = center * lax.rsqrt(jnp.mean(center * center, axis=-1, keepdims=True) + epsilon)
    return normed * (1.0 + scale) + shift


def product(left, right):
    return jnp.dot(left, right, preferred_element_type=jnp.float32)


def contract_rows(left, right):
    return lax.dot_general(
        left, right, (((0,), (0,)), ((), ())), preferred_element_type=jnp.float32
    )


def times_transposed(left, right):
    return lax.dot_general(
        left, right, (((1,), (1,)), ((), ())), preferred_element_type=jnp.float32
    )


def split_heads(values):
    rows = values.shape[0]
    grouped = values.reshape(rows, HEADS // group_heads, group_heads, HEAD_DIM)
    return grouped.transpose(1, 2, 0, 3)


def join_heads(values):
    groups, inner, rows, depth = values.shape
    return values.transpose(2, 0, 1, 3).reshape(rows, groups * inner * depth)


def scores_of(query_group, key_group, valid):
    scores = jnp.einsum(
        "hqd,hkd->hqk", query_group, key_group, preferred_element_type=jnp.float32
    ) * HEAD_DIM ** (-0.5)
    return jnp.where(valid[None, None, :], scores, -1000000000.0)


def attend_forward(query, key_rows, value_rows, valid):

    def one_group(pieces):
        query_group, key_group, value_group = pieces
        scores = scores_of(query_group, key_group, valid)
        top = jnp.max(scores, axis=-1, keepdims=True)
        expo = jnp.exp(scores - top)
        total = jnp.sum(expo, axis=-1, keepdims=True)
        probs = (expo / total).astype(jnp.bfloat16)
        result = jnp.einsum("hqk,hkd->hqd", probs, value_group, preferred_element_type=jnp.float32)
        return (result, top, total)

    results, tops, totals = lax.map(
        one_group, (split_heads(query), split_heads(key_rows), split_heads(value_rows))
    )
    return (join_heads(results), (tops, totals))


def attend_backward(query, key_rows, value_rows, valid, stats, grad_output):
    tops, totals = stats

    def one_group(pieces):
        query_group, key_group, value_group, top, total, grad_group = pieces
        scores = scores_of(query_group, key_group, valid)
        probs = jnp.exp(scores - top) / total
        grad_probs = jnp.einsum(
            "hqd,hkd->hqk", grad_group, value_group, preferred_element_type=jnp.float32
        )
        inner = jnp.sum(probs * grad_probs, axis=-1, keepdims=True)
        grad_scores = (probs * (grad_probs - inner)).astype(jnp.bfloat16)
        factor = HEAD_DIM ** (-0.5)
        grad_query = (
            jnp.einsum("hqk,hkd->hqd", grad_scores, key_group, preferred_element_type=jnp.float32)
            * factor
        )
        grad_keys = (
            jnp.einsum("hqk,hqd->hkd", grad_scores, query_group, preferred_element_type=jnp.float32)
            * factor
        )
        grad_values = jnp.einsum(
            "hqk,hqd->hkd",
            probs.astype(jnp.bfloat16),
            grad_group,
            preferred_element_type=jnp.float32,
        )
        return (grad_query, inner, grad_keys, grad_values)

    results = lax.map(
        one_group,
        (
            split_heads(query),
            split_heads(key_rows),
            split_heads(value_rows),
            tops,
            totals,
            split_heads(grad_output),
        ),
    )
    return (join_heads(results[0]), results[1], join_heads(results[2]), join_heads(results[3]))


def local(
    tokens,
    cotangent,
    image_tokens,
    image_lengths,
    key_mask,
    camera,
    modulation,
    q_cross,
    kv_image,
    out_cross,
    qkv_self,
    out_self,
    mlp_in,
    mlp_out,
):
    q_full, kv_full, out_cross_full, qkv_full, out_self_full, mlp_in_full, mlp_out_full = (
        lax.all_gather(q_cross, "batch", axis=0, tiled=True),
        lax.all_gather(kv_image, "batch", axis=0, tiled=True),
        lax.all_gather(out_cross, "batch", axis=0, tiled=True),
        lax.all_gather(qkv_self, "batch", axis=0, tiled=True),
        lax.all_gather(out_self, "batch", axis=0, tiled=True),
        lax.all_gather(mlp_in, "batch", axis=0, tiled=True),
        lax.all_gather(mlp_out, "batch", axis=0, tiled=True),
    )
    camera_gate = jax.nn.silu(camera.astype(jnp.float32)).astype(jnp.bfloat16)
    modulation_all = lax.psum(product(camera_gate, modulation), "batch")
    object_index = lax.axis_index("batch")
    width = tokens.shape[2]
    shifts = lax.dynamic_index_in_dim(modulation_all, object_index, 0, keepdims=False).reshape(
        6, width
    )
    stream = tokens[0].astype(jnp.float32)
    image_rows = image_tokens[0]
    positions = jnp.arange(image_rows.shape[0], dtype=jnp.int32)
    valid = (positions < image_lengths[0]) & ((key_mask[0] == 1) | (positions == 0))
    everywhere = jnp.ones((lax.axis_size("seq") * stream.shape[0],), dtype=jnp.bool_)
    normed_cross, cross_pullback = jax.vjp(modulated_norm, stream, shifts[0], shifts[1])
    normed_cross = normed_cross.astype(jnp.bfloat16)
    query_cross = product(normed_cross, q_full).astype(jnp.bfloat16)
    image_kv = product(image_rows, kv_full)
    image_keys = image_kv[:, :width].astype(jnp.bfloat16)
    image_values = image_kv[:, width:].astype(jnp.bfloat16)
    attended_cross, cross_stats = attend_forward(query_cross, image_keys, image_values, valid)
    attended_cross = attended_cross.astype(jnp.bfloat16)
    after_cross = stream + product(attended_cross, out_cross_full)
    normed_self, self_pullback = jax.vjp(modulated_norm, after_cross, shifts[2], shifts[3])
    normed_self = normed_self.astype(jnp.bfloat16)
    packed = product(normed_self, qkv_full).astype(jnp.bfloat16)
    query_self = packed[:, :width]
    key_local = packed[:, width : 2 * width]
    value_local = packed[:, 2 * width :]
    key_whole, value_whole = (
        lax.all_gather(key_local, "seq", axis=0, tiled=True),
        lax.all_gather(value_local, "seq", axis=0, tiled=True),
    )
    attended_self, self_stats = attend_forward(query_self, key_whole, value_whole, everywhere)
    attended_self = attended_self.astype(jnp.bfloat16)
    after_self = after_cross + product(attended_self, out_self_full)
    normed_mlp, mlp_pullback = jax.vjp(modulated_norm, after_self, shifts[4], shifts[5])
    normed_mlp = normed_mlp.astype(jnp.bfloat16)
    up_rows = product(normed_mlp, mlp_in_full)
    hidden, gelu_pullback = jax.vjp(jax.nn.gelu, up_rows)
    hidden = hidden.astype(jnp.bfloat16)
    output = after_self + product(hidden, mlp_out_full)
    grad_stream = cotangent[0].astype(jnp.float32)
    grad_branch = grad_stream.astype(jnp.bfloat16)
    grad_mlp_out = contract_rows(hidden, grad_branch)
    (grad_up,) = gelu_pullback(times_transposed(grad_branch, mlp_out_full))
    grad_up = grad_up.astype(jnp.bfloat16)
    grad_mlp_in = contract_rows(normed_mlp, grad_up)
    grad_from, shift_mlp, scale_mlp = mlp_pullback(times_transposed(grad_up, mlp_in_full))
    grad_stream = grad_stream + grad_from
    grad_branch = grad_stream.astype(jnp.bfloat16)
    grad_out_self = contract_rows(attended_self, grad_branch)
    grad_attended = times_transposed(grad_branch, out_self_full).astype(jnp.bfloat16)
    grad_query, inner_local, key_terms, value_terms = attend_backward(
        query_self, key_whole, value_whole, everywhere, self_stats, grad_attended
    )
    grad_key, grad_value = (
        lax.psum_scatter(key_terms, "seq", scatter_dimension=0, tiled=True),
        lax.psum_scatter(value_terms, "seq", scatter_dimension=0, tiled=True),
    )
    grad_packed = jnp.concatenate([grad_query, grad_key, grad_value], axis=1).astype(jnp.bfloat16)
    grad_qkv_self = contract_rows(normed_self, grad_packed)
    grad_from, shift_self, scale_self = self_pullback(times_transposed(grad_packed, qkv_full))
    grad_stream = grad_stream + grad_from
    grad_branch = grad_stream.astype(jnp.bfloat16)
    grad_out_cross = contract_rows(attended_cross, grad_branch)
    grad_attended = times_transposed(grad_branch, out_cross_full).astype(jnp.bfloat16)
    grad_query, inner_cross, key_terms, value_terms = attend_backward(
        query_cross, image_keys, image_values, valid, cross_stats, grad_attended
    )
    image_float = image_rows.astype(jnp.float32)
    image_key_grad, image_value_grad = (
        lax.psum_scatter(
            key_terms.astype(jnp.bfloat16), "seq", scatter_dimension=1, tiled=True
        ).astype(jnp.float32),
        lax.psum_scatter(
            value_terms.astype(jnp.bfloat16), "seq", scatter_dimension=1, tiled=True
        ).astype(jnp.float32),
    )
    block_width = image_key_grad.shape[1]
    column_start = lax.axis_index("seq") * block_width
    image_grads = jnp.concatenate([image_key_grad, image_value_grad], axis=1)
    kv_block = lax.dot_general(
        image_float,
        image_grads,
        (((0,), (0,)), ((), ())),
        precision=highest,
        preferred_element_type=jnp.float32,
    )
    grad_kv_image = jnp.zeros((image_rows.shape[1], 2 * width), jnp.float32)
    grad_kv_image = lax.dynamic_update_slice(
        grad_kv_image, kv_block[:, :block_width], (jnp.int32(0), column_start)
    )
    grad_kv_image = lax.dynamic_update_slice(
        grad_kv_image, kv_block[:, block_width:], (jnp.int32(0), column_start + width)
    )
    grad_query = grad_query.astype(jnp.bfloat16)
    grad_q_cross = contract_rows(normed_cross, grad_query)
    grad_from, shift_cross, scale_cross = cross_pullback(times_transposed(grad_query, q_full))
    grad_input = grad_stream + grad_from
    grad_row = jnp.concatenate(
        [shift_cross, scale_cross, shift_self, scale_self, shift_mlp, scale_mlp]
    )
    grad_table = lax.dynamic_update_slice(
        jnp.zeros(modulation_all.shape, jnp.float32),
        grad_row[None, :],
        (object_index, jnp.int32(0)),
    )
    grad_table = lax.psum(grad_table, ("batch", "seq"))
    grad_modulation = lax.dot_general(
        camera_gate.astype(jnp.float32),
        grad_table,
        (((0,), (0,)), ((), ())),
        precision=highest,
        preferred_element_type=jnp.float32,
    )
    terms = (
        grad_q_cross,
        grad_kv_image,
        grad_out_cross,
        grad_qkv_self,
        grad_out_self,
        grad_mlp_in,
        grad_mlp_out,
    )
    shares = (
        lax.psum_scatter(
            terms[0].astype(jnp.bfloat16), "batch", scatter_dimension=0, tiled=True
        ).astype(jnp.float32),
        lax.psum_scatter(
            terms[1].astype(jnp.bfloat16), "batch", scatter_dimension=0, tiled=True
        ).astype(jnp.float32),
        lax.psum_scatter(
            terms[2].astype(jnp.bfloat16), "batch", scatter_dimension=0, tiled=True
        ).astype(jnp.float32),
        lax.psum_scatter(
            terms[3].astype(jnp.bfloat16), "batch", scatter_dimension=0, tiled=True
        ).astype(jnp.float32),
        lax.psum_scatter(
            terms[4].astype(jnp.bfloat16), "batch", scatter_dimension=0, tiled=True
        ).astype(jnp.float32),
        lax.psum_scatter(
            terms[5].astype(jnp.bfloat16), "batch", scatter_dimension=0, tiled=True
        ).astype(jnp.float32),
        lax.psum_scatter(
            terms[6].astype(jnp.bfloat16), "batch", scatter_dimension=0, tiled=True
        ).astype(jnp.float32),
    )
    totals = (
        lax.psum(shares[0].astype(jnp.bfloat16), "seq").astype(jnp.float32),
        lax.psum(shares[1].astype(jnp.bfloat16), "seq").astype(jnp.float32),
        lax.psum(shares[2].astype(jnp.bfloat16), "seq").astype(jnp.float32),
        lax.psum(shares[3].astype(jnp.bfloat16), "seq").astype(jnp.float32),
        lax.psum(shares[4].astype(jnp.bfloat16), "seq").astype(jnp.float32),
        lax.psum(shares[5].astype(jnp.bfloat16), "seq").astype(jnp.float32),
        lax.psum(shares[6].astype(jnp.bfloat16), "seq").astype(jnp.float32),
    )
    return (
        output.astype(jnp.bfloat16)[None],
        grad_input[None],
        grad_modulation,
        totals[0],
        totals[1],
        totals[2],
        totals[3],
        totals[4],
        totals[5],
        totals[6],
    )


bf16 = jnp.bfloat16
f32 = jnp.float32
MESH = pl.DeviceIdType.MESH
BELOW = -3.0e38


def nn(a, b):
    return jnp.dot(a, b, preferred_element_type=f32)


def nt(a, b):
    return lax.dot_general(a, b, (((1,), (1,)), ((), ())), preferred_element_type=f32)


def tn(a, b):
    return lax.dot_general(a, b, (((0,), (0,)), ((), ())), preferred_element_type=f32)


def one_head(pair, side):
    lane = lax.broadcasted_iota(jnp.int32, pair.shape, 1)
    return jnp.where(lane // HEAD_DIM == side, pair, jnp.zeros_like(pair))


def two_heads(first, second):
    lane = lax.broadcasted_iota(jnp.int32, first.shape, 1)
    return jnp.where(lane < HEAD_DIM, first, second)


def softmax_rows(scores, mask):
    if mask is not None:
        scores = jnp.where(mask[0:1, :] > 0.5, scores, mask[1:2, :])
    expo = jnp.exp(scores - jnp.max(scores, axis=-1, keepdims=True))
    return expo * (1.0 / jnp.sum(expo, axis=-1, keepdims=True))


def norm_stats(rows):
    center = rows - jnp.mean(rows, axis=-1, keepdims=True)
    inverse = lax.rsqrt(jnp.mean(center * center, axis=-1, keepdims=True) + epsilon)
    return center * inverse, inverse


def norm_forward(rows, shift, scale):
    return norm_stats(rows)[0] * (1.0 + scale) + shift


def norm_backward(rows, scale, grad):
    normed, inverse = norm_stats(rows)
    inner = grad * (1.0 + scale)
    mean_inner = jnp.mean(inner, axis=-1, keepdims=True)
    mean_cross = jnp.mean(inner * normed, axis=-1, keepdims=True)
    grad_rows = inverse * (inner - mean_inner - normed * mean_cross)
    return (
        grad_rows,
        jnp.sum(grad, axis=0, keepdims=True),
        jnp.sum(grad * normed, axis=0, keepdims=True),
    )


Q, KV, OC, QKV, OS, UP, DOWN, CAMERA, TABLE, TOKENS, OWN, IMAGE, COTANGENT = range(13)


GATHER = (
    (KV, 0, 1),
    (Q, 0, 1),
    (OC, 0, 1),
    (QKV, 0, 2),
    (QKV, 1, 2),
    (OS, 0, 1),
    (UP, 0, 4),
    (UP, 1, 4),
    (UP, 2, 4),
    (UP, 3, 4),
    (DOWN, 0, 4),
    (DOWN, 1, 4),
    (DOWN, 2, 4),
    (DOWN, 3, 4),
)
SCATTER = (
    (DOWN, 0, 4),
    (DOWN, 1, 4),
    (DOWN, 2, 4),
    (DOWN, 3, 4),
    (UP, 0, 4),
    (UP, 1, 4),
    (UP, 2, 4),
    (UP, 3, 4),
    (OS, 0, 1),
    (QKV, 0, 2),
    (QKV, 1, 2),
    (OC, 0, 1),
    (Q, 0, 1),
    (KV, 0, 1),
)
BY_ROWS = (OC, OS)
AHEAD = 2


class Sizes:
    def __init__(self, mesh_shape, inputs):
        self.batch, self.seq = mesh_shape["batch"], mesh_shape["seq"]
        self.own, self.width = inputs[0].shape[1:]
        self.image_rows, self.image_width = inputs[2].shape[1:]
        self.chunks = 4
        self.part = self.own // self.chunks
        self.rows = self.seq * self.part
        self.tokens = self.seq * self.own
        self.columns = self.width // self.seq
        self.hidden = inputs[12].shape[1] // self.seq
        self.keys = -(-self.image_rows // 128) * 128
        self.whole_rows = self.image_rows // 128 * 128
        self.block = self.width // self.batch
        self.image_block = self.image_width // self.batch
        self.weights = (
            (self.block, self.columns),
            (self.image_block, 2 * self.columns),
            (self.block // self.seq, self.width),
            (self.block, 3 * self.columns),
            (self.block // self.seq, self.width),
            (self.block, self.hidden),
            (self.hidden // self.batch, self.width),
        )


class Refs:
    def __init__(self, refs):
        rest = iter(refs)
        self.tokens = next(rest)
        self.cotangent = next(rest)
        self.image = next(rest)
        self.marks = next(rest)
        self.lengths = next(rest)
        self.camera = next(rest)
        self.modulation = next(rest)
        self.q_cross = next(rest)
        self.kv_image = next(rest)
        self.out_cross = next(rest)
        self.qkv_self = next(rest)
        self.out_self = next(rest)
        self.mlp_in = next(rest)
        self.mlp_out = next(rest)
        self.output = next(rest)
        self.grad_tokens = next(rest)
        self.table = next(rest)
        self.gout = [next(rest) for _ in range(7)]
        self.weights = [next(rest) for _ in range(7)]
        self.firsts = [next(rest) for _ in range(7)]
        self.seconds = [next(rest) for _ in range(7)]
        self.buf_a = next(rest)
        self.buf_b = next(rest)
        self.buf_h2 = next(rest)
        self.buf_b2 = next(rest)
        self.part_main = next(rest)
        self.core_main = next(rest)
        self.send_main = next(rest)
        self.line_main = next(rest)
        self.part_side = next(rest)
        self.core_side = next(rest)
        self.send_side = next(rest)
        self.line_side = next(rest)
        self.turn_in = [next(rest) for _ in range(2)]
        self.turn_out = [next(rest) for _ in range(2)]
        self.image_all = next(rest)
        self.tail = next(rest)
        self.marks_own = next(rest)
        self.mask_all = next(rest)
        self.camera_own = next(rest)
        self.mods_all = next(rest)
        self.mods = next(rest)
        self.sums = next(rest)
        self.sums_seq = next(rest)
        self.normed1 = next(rest)
        self.query1 = next(rest)
        self.key1 = next(rest)
        self.value1 = next(rest)
        self.att1 = next(rest)
        self.packed2 = next(rest)
        self.att2 = next(rest)
        self.hidden = next(rest)
        self.grad_up = next(rest)
        self.grad_key = next(rest)
        self.grad_value = next(rest)
        self.x0 = next(rest)
        self.x1 = next(rest)
        self.x2 = next(rest)
        self.dx = next(rest)
        self.grads_a = next(rest)
        self.grads_b = next(rest)
        self.grads_c = next(rest)
        self.sem_load = next(rest)
        self.sem_wz_s = next(rest)
        self.sem_wz_r = next(rest)
        self.sem_wx_s = next(rest)
        self.sem_wx_r = next(rest)
        self.sem_gx_s = next(rest)
        self.sem_gx_r = next(rest)
        self.sem_gz_s = next(rest)
        self.sem_gz_r = next(rest)
        self.sem_gs_s = next(rest)
        self.sem_gs_r = next(rest)
        self.sem_own = next(rest)
        self.sem_ti_s = next(rest)
        self.sem_ti_r = next(rest)
        self.sem_to_s = next(rest)
        self.sem_to_r = next(rest)
        self.sem_in_s = next(rest)
        self.sem_in_r = next(rest)
        self.sem_ag_s = next(rest)
        self.sem_ag_r = next(rest)
        self.sem_rs_s = next(rest)
        self.sem_rs_r = next(rest)
        self.sem_m_s = next(rest)
        self.sem_m_r = next(rest)
        self.sem_d_s = next(rest)
        self.sem_d_r = next(rest)
        self.sem_t_s = next(rest)
        self.sem_t_r = next(rest)
        self.sem_out = next(rest)


def whole_layer(z, *refs):
    r = Refs(refs)
    W, FIRST, SECOND, GOUT = r.weights, r.firsts, r.seconds, r.gout
    n, S, B = z.chunks, z.seq, z.batch
    part, rows, D, C = z.part, z.rows, z.width, z.columns
    Z = B // 2
    b = lax.axis_index("batch")
    s = lax.axis_index("seq")
    zz = b // 2
    x = lax.rem(b, 2)
    y = s // 2
    c = lax.rem(s, 2)
    other_x = 1 - x
    other_c = 1 - c
    other_y = 1 - y
    x_peer = (2 * zz + other_x, s)
    core_peer = (b, 2 * y + other_c)
    line_peer = (b, 2 * other_y + c)
    line_slot = 2 * other_y + c
    core_slot = 2 * y + other_c
    far_slot = 2 * other_y + other_c

    def z_of(j):
        return lax.rem(zz + j, Z)

    def remote(src, dst, send, recv, device):
        return pltpu.make_async_remote_copy(
            src_ref=src,
            dst_ref=dst,
            send_sem=send,
            recv_sem=recv,
            device_id=device,
            device_id_type=MESH,
        )

    def arrived(dst, send, recv, device):
        remote(dst, dst, send, recv, device).wait_recv()

    barrier = pltpu.get_barrier_semaphore()
    for j in range(1, B):
        pl.semaphore_signal(barrier, inc=1, device_id=(lax.rem(b + j, B), s), device_id_type=MESH)
    for j in range(1, S):
        pl.semaphore_signal(barrier, inc=1, device_id=(b, lax.rem(s + j, S)), device_id_type=MESH)

    loads = {}

    def load(key, src, dst):
        count = sum(len(copies) for copies in loads.values())
        copy = pltpu.make_async_copy(src, dst, r.sem_load.at[count])
        loads.setdefault(key, []).append(copy)
        copy.start()

    def col(index, width):
        return pl.ds(pl.multiple_of(index * width, 128), width)

    wide = z.hidden // B
    for j in range(2):
        load(
            KV,
            r.kv_image.at[:, pl.ds(pl.multiple_of(j * D + s * C, 128), C)],
            W[KV].at[b, :, pl.ds(j * C, C)],
        )
    load(Q, r.q_cross.at[:, col(s, C)], W[Q].at[b])
    load(TOKENS, r.tokens, r.buf_a.at[:, s])
    load(CAMERA, r.camera, r.camera_own)
    for k in range(6):
        load(TABLE, r.modulation.at[:, pl.ds(k * D, D)], r.hidden.at[pl.ds(k * z.block, z.block)])
    few = z.block // S
    load(OC, r.out_cross.at[pl.ds(pl.multiple_of(s * few, 16), few)], r.turn_in[0].at[zz])
    for j in range(3):
        load(
            QKV,
            r.qkv_self.at[:, pl.ds(pl.multiple_of(j * D + s * C, 128), C)],
            W[QKV].at[b, :, pl.ds(j * C, C)],
        )
    load(OS, r.out_self.at[pl.ds(pl.multiple_of(s * few, 16), few)], r.turn_in[1].at[zz])
    load(IMAGE, r.image, r.image_all)
    load(IMAGE, r.marks, r.marks_own)
    for j in range(B):
        load(
            UP,
            r.mlp_in.at[:, pl.ds(pl.multiple_of(j * (z.hidden * S // B) + s * wide, 128), wide)],
            W[UP].at[b, :, pl.ds(j * wide, wide)],
        )
    load(DOWN, r.mlp_out.at[pl.ds(pl.multiple_of(s * wide, 128), wide), :], W[DOWN].at[b])
    load(COTANGENT, r.cotangent, r.buf_b.at[:, s])
    load(OWN, r.tokens, r.x0)

    pl.semaphore_wait(barrier, B - 1 + S - 1)

    def loaded(key):
        for copy in loads[key]:
            copy.wait()

    def rows_of(piece):
        w, which, parts = piece
        count = z.weights[w][0] // parts
        return w, pl.ds(which * count, count)

    def turned(w):
        return 0 if w == OC else 1

    def quarter(index):
        return pl.ds(pl.multiple_of(index * few, 16), few)

    def z_place(k, from_z):
        w, span = rows_of(GATHER[k])
        return r.turn_in[turned(w)].at[from_z] if w in BY_ROWS else W[w].at[2 * from_z + x, span]

    def z_send(k, j):
        place = z_place(k, zz)
        return remote(
            place, place, r.sem_wz_s.at[k, j - 1], r.sem_wz_r.at[k, zz], (2 * z_of(j) + x, s)
        )

    def x_send(k, from_z):
        w, span = rows_of(GATHER[k])
        place, mark = (W[w].at[x], 0) if w in BY_ROWS else (z_place(k, from_z), from_z)
        return remote(place, place, r.sem_wx_s.at[k, mark], r.sem_wx_r.at[k, mark], x_peer)

    def turn_send(w, j):
        to = lax.rem(s + j, S)
        return remote(
            r.turn_in[turned(w)].at[to],
            W[w].at[x, quarter(s)],
            r.sem_ti_s.at[turned(w), j - 1],
            r.sem_ti_r.at[turned(w), s],
            (b, to),
        )

    def z_near(j):
        return (zz != Z - 1) if j == 1 else (zz != 0)

    def z_far(k):
        place = z_place(k, z_of(2))
        return remote(
            place,
            place,
            r.sem_wz_s.at[k, Z - 1],
            r.sem_wz_r.at[k, z_of(2)],
            (2 * (Z - 1) * (zz - 1) + x, s),
        )

    def between():
        return (zz == 1) | (zz == 2)

    def weight_start(k):
        if k >= len(GATHER):
            return
        w, which, _ = GATHER[k]
        if which == 0:
            loaded(w)
        z_send(k, 2).start()
        for j in (1, 3):
            pl.when(z_near(j))(z_send(k, j).start)
        if w not in BY_ROWS:
            x_send(k, zz).start()

    def weight_came(k, j):
        w, _ = rows_of(GATHER[k])
        from_z = z_of(j)
        arrived(
            z_place(k, from_z), r.sem_wz_s.at[k, 0], r.sem_wz_r.at[k, from_z], (2 * from_z + x, s)
        )
        if w not in BY_ROWS:
            x_send(k, from_z).start()

    def weight_far(k):
        for j in (1, 3):
            pl.when(jnp.logical_not(z_near(j)))(functools.partial(weight_came, k, j))

    def weight_pass(k):
        w, _ = rows_of(GATHER[k])
        weight_came(k, 2)
        pl.when(between())(z_far(k).start)
        for j in (1, 3):
            pl.when(z_near(j))(functools.partial(weight_came, k, j))
        weight_start(k + AHEAD)
        if k and GATHER[k - 1][0] not in BY_ROWS:
            weight_far(k - 1)
        if w in BY_ROWS:
            weight_far(k)
            for j in range(1, S):
                turn_send(w, j).start()
            W[w][x, quarter(s), :] = r.turn_in[turned(w)][s]

    def weight_turn(k):
        w, _ = rows_of(GATHER[k])
        for j in range(1, S):
            m = lax.rem(s + j, S)
            arrived(
                W[w].at[x, quarter(m)], r.sem_ti_s.at[turned(w), 0], r.sem_ti_r.at[turned(w), m], (b, m)
            )
        x_send(k, zz).start()

    def weight_wait(w):
        for k in range(len(GATHER)):
            if GATHER[k][0] != w:
                continue
            _, span = rows_of(GATHER[k])
            if w in BY_ROWS:
                arrived(W[w].at[other_x], r.sem_wx_s.at[k, 0], r.sem_wx_r.at[k, 0], x_peer)
                continue
            for from_z in range(Z):
                place = W[w].at[2 * from_z + other_x, span]
                arrived(place, r.sem_wx_s.at[k, 0], r.sem_wx_r.at[k, from_z], x_peer)

    def weight_drain(k):
        w, _ = rows_of(GATHER[k])
        z_send(k, 2).wait_send()
        for j in (1, 3):
            pl.when(z_near(j))(z_send(k, j).wait_send)
        pl.when(between())(z_far(k).wait_send)
        if w in BY_ROWS:
            x_send(k, zz).wait_send()
            for j in range(1, S):
                turn_send(w, j).wait_send()
        else:
            for j in range(Z):
                x_send(k, z_of(j)).wait_send()

    def give(buf, i, k):
        slot, peer = [(s, core_peer), (s, line_peer), (line_slot, core_peer)][k]
        return remote(
            buf.at[i, slot], buf.at[i, slot], r.sem_ag_s.at[i, k], r.sem_ag_r.at[i, k], peer
        )

    def gather_start(buf, i):
        give(buf, i, 1).start()
        give(buf, i, 0).start()

    def gather_pass(buf, i):
        arrived(buf.at[i, line_slot], r.sem_ag_s.at[i, 1], r.sem_ag_r.at[i, 1], line_peer)
        give(buf, i, 2).start()

    def gather_wait(buf, i):
        arrived(buf.at[i, core_slot], r.sem_ag_s.at[i, 0], r.sem_ag_r.at[i, 0], core_peer)
        arrived(buf.at[i, far_slot], r.sem_ag_s.at[i, 2], r.sem_ag_r.at[i, 2], core_peer)
        for k in range(3):
            give(buf, i, k).wait_send()

    def give_input(buf, m, k):
        slot, peer = [(s, core_peer), (s, line_peer), (line_slot, core_peer)][k]
        return remote(
            buf.at[:, slot], buf.at[:, slot], r.sem_in_s.at[m, k], r.sem_in_r.at[m, k], peer
        )

    def input_start(buf, m):
        give_input(buf, m, 1).start()
        give_input(buf, m, 0).start()

    def input_pass(buf, m):
        arrived(buf.at[:, line_slot], r.sem_in_s.at[m, 1], r.sem_in_r.at[m, 1], line_peer)
        give_input(buf, m, 2).start()

    def input_wait(buf, m):
        arrived(buf.at[:, core_slot], r.sem_in_s.at[m, 0], r.sem_in_r.at[m, 0], core_peer)
        arrived(buf.at[:, far_slot], r.sem_in_s.at[m, 2], r.sem_in_r.at[m, 2], core_peer)
        for k in range(3):
            give_input(buf, m, k).wait_send()

    lanes = (
        (r.part_main, r.core_main, r.send_main, r.line_main),
        (r.part_side, r.core_side, r.send_side, r.line_side),
    )

    def sum_core(lane, i):
        mine, core, _, _ = lanes[lane]
        return remote(
            mine.at[i, :, other_c],
            core.at[i],
            r.sem_rs_s.at[lane, i, 0],
            r.sem_rs_r.at[lane, i, 0],
            core_peer,
        )

    def sum_line(lane, i):
        _, _, send, line = lanes[lane]
        return remote(
            send.at[i],
            line.at[i],
            r.sem_rs_s.at[lane, i, 1],
            r.sem_rs_r.at[lane, i, 1],
            line_peer,
        )

    def sum_start(lane, i, value):
        lanes[lane][0][i] = value.astype(bf16).reshape(2, 2, part, D)
        sum_core(lane, i).start()

    def sum_pass(lane, i):
        mine, core, send, _ = lanes[lane]
        sum_core(lane, i).wait_recv()
        send[i] = (mine[i, other_y, c].astype(f32) + core[i, other_y].astype(f32)).astype(bf16)
        sum_line(lane, i).start()

    def sum_end(lane, i):
        mine, core, _, line = lanes[lane]
        sum_line(lane, i).wait_recv()
        total = mine[i, y, c].astype(f32) + core[i, y].astype(f32) + line[i].astype(f32)
        sum_core(lane, i).wait_send()
        sum_line(lane, i).wait_send()
        return total

    def grad_place(w):
        return {
            Q: r.grads_a.at[:, :, :, pl.ds(0, C)],
            KV: r.grads_a.at[:, :, pl.ds(0, z.image_block), pl.ds(C, 2 * C)],
            OC: r.grads_c.at[0],
            QKV: r.grads_b.at[:, :, :, pl.ds(0, 3 * C)],
            OS: r.grads_c.at[1],
            UP: r.grads_a,
            DOWN: r.grads_b,
        }[w]

    def first_of(k):
        w, span = rows_of(SCATTER[k])
        return r.turn_out[turned(w)].at[zz] if w in BY_ROWS else FIRST[w].at[zz, span]

    def grad_x(k):
        w, span = rows_of(SCATTER[k])
        place = grad_place(w)
        src = place.at[other_x] if w in BY_ROWS else place.at[:, other_x, span]
        dst = FIRST[w] if w in BY_ROWS else FIRST[w].at[:, span]
        return remote(src, dst, r.sem_gx_s.at[k], r.sem_gx_r.at[k], x_peer)

    def turn_back(w, j):
        to = lax.rem(s + j, S)
        return remote(
            FIRST[w].at[quarter(to)],
            r.turn_out[turned(w)].at[s],
            r.sem_to_s.at[turned(w), j - 1],
            r.sem_to_r.at[turned(w), s],
            (b, to),
        )

    def grad_z(k, j):
        w, span = rows_of(SCATTER[k])
        to = z_of(j)
        src = r.turn_out[turned(w)].at[to] if w in BY_ROWS else FIRST[w].at[to, span]
        return remote(
            src,
            SECOND[w].at[Z - j - 1, span],
            r.sem_gz_s.at[k, j - 1],
            r.sem_gz_r.at[k, zz],
            (2 * to + x, s),
        )

    def shared(k, origin):
        w, span = rows_of(SCATTER[k])
        return GOUT[w].at[origin, span]

    def grad_s(k, way):
        mine = shared(k, line_slot) if way == 2 else first_of(k)
        origin = line_slot if way == 2 else s
        peer = line_peer if way == 1 else core_peer
        return remote(mine, shared(k, origin), r.sem_gs_s.at[k, way], r.sem_gs_r.at[k, way], peer)

    def grad_own(k):
        return pltpu.make_async_copy(first_of(k), shared(k, s), r.sem_own.at[k])

    def grad_relay(k):
        arrived(shared(k, line_slot), r.sem_gs_s.at[k, 1], r.sem_gs_r.at[k, 1], line_peer)
        grad_s(k, 2).start()

    def grad_start(k):
        grad_x(k).start()

    def grad_pass(k):
        w, span = rows_of(SCATTER[k])
        grad_x(k).wait_recv()
        place = grad_place(w)
        if w in BY_ROWS:
            FIRST[w][...] = (FIRST[w][...].astype(f32) + place[x].astype(f32)).astype(bf16)
            for j in range(1, S):
                turn_back(w, j).start()
            r.turn_out[turned(w)][s] = FIRST[w][quarter(s), :]
        else:
            for m in range(Z):
                term = FIRST[w][m, span].astype(f32) + place[m, x, span].astype(f32)
                FIRST[w][m, span] = term.astype(bf16)
            for j in range(1, Z):
                grad_z(k, j).start()
        grad_x(k).wait_send()

    def grad_turn(k):
        w, _ = rows_of(SCATTER[k])
        for j in range(1, S):
            m = lax.rem(s + j, S)
            arrived(
                r.turn_out[turned(w)].at[m],
                r.sem_to_s.at[turned(w), 0],
                r.sem_to_r.at[turned(w), m],
                (b, m),
            )
        for j in range(1, Z):
            grad_z(k, j).start()

    def grad_end(k):
        w, span = rows_of(SCATTER[k])
        mine = first_of(k)
        total = mine[...].astype(f32)
        for j in range(1, Z):
            m = z_of(j)
            term = SECOND[w].at[j - 1, span]
            arrived(term, r.sem_gz_s.at[k, 0], r.sem_gz_r.at[k, m], (2 * m + x, s))
            total = total + term[...].astype(f32)
        mine[...] = total.astype(bf16)
        grad_s(k, 1).start()
        grad_s(k, 0).start()
        grad_own(k).start()
        for j in range(1, Z):
            grad_z(k, j).wait_send()

    def grad_drain(k):
        w, _ = rows_of(SCATTER[k])
        arrived(shared(k, core_slot), r.sem_gs_s.at[k, 0], r.sem_gs_r.at[k, 0], core_peer)
        arrived(shared(k, far_slot), r.sem_gs_s.at[k, 2], r.sem_gs_r.at[k, 2], core_peer)
        for way in range(3):
            grad_s(k, way).wait_send()
        grad_own(k).wait()
        if w in BY_ROWS:
            for j in range(1, S):
                turn_back(w, j).wait_send()

    def mods_send(j):
        to = lax.rem(b + j, B)
        return remote(
            r.x2.at[0, pl.ds(pl.multiple_of(8 * to, 8), 8)],
            r.mods_all.at[b],
            r.sem_m_s.at[j - 1],
            r.sem_m_r.at[b],
            (to, s),
        )

    for k in range(AHEAD):
        weight_start(k)
    loaded(TOKENS)
    input_start(r.buf_a, 0)
    loaded(CAMERA)
    loaded(TABLE)
    camera = r.camera_own[...].astype(f32)
    gate = (camera * jax.nn.sigmoid(camera)).astype(bf16)
    for k in range(6):
        term = nn(gate, r.hidden[k * z.block : (k + 1) * z.block, :])
        for o in range(B):
            r.x2[0, 8 * o + k : 8 * o + k + 1, :] = term[o : o + 1, :]
    for j in range(1, B):
        mods_send(j).start()
    loaded(COTANGENT)
    input_start(r.buf_b, 1)
    loaded(IMAGE)
    loaded(OWN)
    places = lax.broadcasted_iota(jnp.int32, (1, z.image_rows), 1)
    valid = (places < r.lengths[0]) & ((r.marks_own[...] == 1) | (places == 0))
    places = lax.broadcasted_iota(jnp.int32, (1, z.keys), 1)
    r.mask_all[0:1, :] = jnp.zeros((1, z.keys), f32)
    r.mask_all[0:1, : z.image_rows] = jnp.where(valid, 1.0, 0.0)
    r.mask_all[1:2, :] = jnp.where(places < z.image_rows, -1000000000.0, BELOW)
    rest = z.image_rows - z.whole_rows
    last = r.image_all[z.whole_rows :, :]
    padding = jnp.zeros((z.keys - z.image_rows, z.image_width), bf16)
    r.tail[...] = jnp.concatenate([last, padding], axis=0) if rest else padding

    mods = r.x2[0, pl.ds(pl.multiple_of(8 * b, 8), 8)]
    for j in range(1, B):
        k = lax.rem(b + j, B)
        arrived(r.mods_all.at[k], r.sem_m_s.at[0], r.sem_m_r.at[k], (k, s))
        mods = mods + r.mods_all[k]
    r.mods[...] = mods
    for j in range(1, B):
        mods_send(j).wait_send()

    def mod(k):
        return r.mods[k : k + 1, :]

    def chunk(i):
        return pl.ds(pl.multiple_of(i * rows, rows), rows)

    scale_q = HEAD_DIM ** (-0.5)
    input_pass(r.buf_a, 0)
    weight_pass(0)
    weight_pass(1)
    input_wait(r.buf_a, 0)

    def normalize(i, _):
        rows_in = r.buf_a[i].reshape(rows, D).astype(f32)
        r.normed1[chunk(i), :] = norm_forward(rows_in, mod(0), mod(1)).astype(bf16)
        return 0

    lax.fori_loop(0, n, normalize, 0)
    weight_wait(KV)

    def project_rows(block, part_rows):
        both = nn(block, W[KV][...].reshape(z.image_width, 2 * C))
        r.key1[part_rows, :] = both[:, :C].astype(bf16)
        r.value1[part_rows, :] = both[:, C:].astype(bf16)

    def project_image(k, _):
        part_rows = pl.ds(pl.multiple_of(k * 128, 128), 128)
        project_rows(r.image_all[part_rows, :], part_rows)
        return 0

    lax.fori_loop(0, z.whole_rows // 128, project_image, 0)
    project_rows(r.tail[...], pl.ds(z.whole_rows, z.keys - z.whole_rows))
    weight_pass(2)
    weight_wait(Q)

    def project_query(i):
        query = nn(r.normed1[chunk(i), :], W[Q][...].reshape(D, C)).astype(bf16)
        r.query1[chunk(i), :] = (query * scale_q).astype(bf16)

    def attend(i, query, key, value, att, mask):
        for p in range(C // 128):
            lane = slice(128 * p, 128 * p + 128)
            pair = query(i, lane)
            keys, values = key(lane), value(lane)
            result = []
            for side in range(2):
                probs = softmax_rows(nt(one_head(pair, side), keys), mask).astype(bf16)
                result.append(nn(probs, values))
            att[chunk(i), lane] = two_heads(*result).astype(bf16)

    def attend_back(i, query, key, value, grad, mask, grad_query):
        query_t = query(i, slice(0, C)).T
        grad_t = grad.T
        for p in range(C // 128):
            lane = slice(128 * p, 128 * p + 128)
            pair, grad_pair = query(i, lane), grad[:, lane]
            keys, values = key(lane), value(lane)
            result = []
            for side in range(2):
                head = slice(128 * p + HEAD_DIM * side, 128 * p + HEAD_DIM * (side + 1))
                probs = softmax_rows(nt(one_head(pair, side), keys), mask)
                grad_probs = nt(one_head(grad_pair, side), values)
                inner = jnp.sum(probs * grad_probs, axis=-1, keepdims=True)
                scores = (probs * (grad_probs - inner)).astype(bf16)
                count = keys.shape[0]
                value_term = nn(grad_t[head, :], probs.astype(bf16))
                key_term = nn(query_t[head, :], scores)
                r.grad_value[head, :count] += value_term
                r.grad_key[head, :count] += key_term
                result.append(nn(scores, keys))
            grad_query[chunk(i), lane] = (two_heads(*result) * scale_q).astype(bf16)

    cross = (
        lambda i, lane: r.query1[chunk(i), lane],
        lambda lane: r.key1[:, lane],
        lambda lane: r.value1[:, lane],
    )

    def plus(lane, offset):
        return slice(lane.start + offset, lane.stop + offset)

    own = (
        lambda i, lane: r.packed2[chunk(i), lane],
        lambda lane: r.packed2[:, plus(lane, C)],
        lambda lane: r.packed2[:, plus(lane, 2 * C)],
    )
    mask_rows = r.mask_all

    def at(i, value, stage):
        pl.when(i == value)(stage)

    def run(calls):
        for call, *values in calls:
            call(*values)

    def pipeline(ticks, *stages):
        last = max(offset for offset, _ in stages)

        def body(step, _):
            for when, calls in ticks.items():
                at(step, when, functools.partial(run, calls))
            for offset, stage in stages:
                i = step - offset

                @pl.when((i >= 0) & (i < n))
                def _():
                    stage(i)

            return 0

        lax.fori_loop(0, n + last, body, 0)

    def cross_forward(i):
        project_query(i)
        attend(i, *cross, r.att1, mask_rows)
        at(i, 0, functools.partial(run, [(weight_turn, 2), (weight_wait, OC)]))
        sum_start(0, i, nn(r.att1[chunk(i), :], W[OC][...].reshape(C, D)))

    def after_cross(i):
        total = r.x0[i].astype(f32) + sum_end(0, i)
        r.x1[i] = total
        r.buf_h2[i, s] = norm_forward(total, mod(2), mod(3)).astype(bf16)
        gather_start(r.buf_h2, i)

    def project_self(i):
        at(i, 0, functools.partial(weight_wait, QKV))
        gather_wait(r.buf_h2, i)
        packed = nn(r.buf_h2[i].reshape(rows, D), W[QKV][...].reshape(D, 3 * C)).astype(bf16)
        r.packed2[chunk(i), :C] = (packed[:, :C] * scale_q).astype(bf16)
        r.packed2[chunk(i), C:] = packed[:, C:]

    pipeline(
        {
            1: [(weight_pass, 3)],
            2: [(weight_pass, 4)],
            3: [(weight_pass, 5)],
            4: [(weight_pass, 6)],
            5: [(weight_turn, 5), (weight_pass, 7)],
            6: [(weight_pass, 8)],
            7: [(weight_pass, 9)],
        },
        (0, cross_forward),
        (1, lambda i: sum_pass(0, i)),
        (2, after_cross),
        (3, lambda i: gather_pass(r.buf_h2, i)),
        (4, project_self),
    )

    weight_wait(OS)
    input_pass(r.buf_b, 1)
    input_wait(r.buf_b, 1)
    r.sums[...] = jnp.zeros_like(r.sums)

    def clear_keys():
        r.grad_key[...] = jnp.zeros_like(r.grad_key)
        r.grad_value[...] = jnp.zeros_like(r.grad_value)

    clear_keys()

    def output_copy(i):
        return pltpu.make_async_copy(
            r.part_side.at[i, 0, 0], r.output.at[i], r.sem_out.at[2 + i]
        )

    def self_forward(i):
        attend(i, *own, r.att2, None)
        sum_start(0, i, nn(r.att2[chunk(i), :], W[OS][...].reshape(C, D)))

    def after_self(i):
        total = r.x1[i] + sum_end(0, i)
        r.x2[i] = total
        r.buf_a[i, s] = norm_forward(total, mod(4), mod(5)).astype(bf16)
        gather_start(r.buf_a, i)

    def feed(i):
        at(i, 0, functools.partial(run, [(weight_far, 13), (weight_wait, UP), (weight_wait, DOWN)]))
        gather_wait(r.buf_a, i)
        rows_in = r.buf_a[i].reshape(rows, D)
        grad_out = r.buf_b[i].reshape(rows, D)
        up = W[UP]
        down = W[DOWN]
        forward = backward = None
        pieces = 2
        wide_piece = z.hidden // pieces
        for k in range(pieces):
            lane = slice(k * wide_piece, (k + 1) * wide_piece)
            up_piece = up[:, :, lane].reshape(D, wide_piece)
            down_piece = down[k * (B // pieces) : (k + 1) * (B // pieces)].reshape(wide_piece, D)
            u = nn(rows_in, up_piece)
            square = u * u
            root = 0.7978845608028654
            tanh = jnp.tanh(root * u * (1.0 + 0.044715 * square))
            half = 0.5 * (1.0 + tanh)
            hidden = (u * half).astype(bf16)
            slope = half + 0.5 * u * (1.0 - tanh * tanh) * (root * (1.0 + 0.134145 * square))
            grad_up = (nt(grad_out, down_piece) * slope).astype(bf16)
            r.hidden[chunk(i), lane] = hidden
            r.grad_up[chunk(i), lane] = grad_up
            first = nn(hidden, down_piece)
            second = nt(grad_up, up_piece)
            forward = first if forward is None else forward + first
            backward = second if backward is None else backward + second
        sum_start(0, i, backward)
        sum_start(1, i, forward)

    def keep_sums(k, shift, scale):
        r.sums[k : k + 1, :] += shift
        r.sums[k + 1 : k + 2, :] += scale

    def after_feed(i):
        stream = r.x2[i]
        grad, shift, scale = norm_backward(stream, mod(5), sum_end(0, i))
        keep_sums(4, shift, scale)
        grad = r.buf_b[i, s].astype(f32) + grad
        r.buf_b2[i, s] = grad.astype(bf16)
        gather_start(r.buf_b2, i)
        r.dx[i] = grad

    def layer_output(i):
        total = r.x2[i] + sum_end(1, i)
        r.part_side[i, 0, 0] = total.astype(bf16)
        output_copy(i).start()

    def self_back(i):
        gather_wait(r.buf_b2, i)
        grad = nt(r.buf_b2[i].reshape(rows, D), W[OS][...].reshape(C, D)).astype(bf16)
        attend_back(i, *own, grad, None, r.grad_up)

    def grads_into(place, lhs, rhs, width):
        def one(o, _):
            value = tn(lhs(col(o, z.block)), rhs()).astype(bf16)
            place[o // 2, lax.rem(o, 2), :, :width] = value
            return 0

        lax.fori_loop(0, B, one, 0)

    def whole(buf):
        return lambda lane: buf[:, :, :, lane].reshape(z.tokens, z.block)

    def feed_grads():
        grads_into(
            r.grads_b,
            lambda lane: r.hidden[:, lane],
            lambda: r.buf_b[...].reshape(z.tokens, D),
            D,
        )
        for k in range(3):
            grad_start(k)
        grads_into(r.grads_a, whole(r.buf_a), lambda: r.grad_up[...], z.hidden)

    pipeline(
        {
            0: [(weight_pass, 10)],
            1: [(weight_pass, 11)],
            2: [(weight_pass, 12)],
            4: [(weight_pass, 13)],
            9: [(grad_pass, 0), (grad_start, 3)],
            10: [(grad_pass, 1), (grad_start, 4)],
            11: [(grad_pass, 2), (grad_start, 5)],
        },
        (0, self_forward),
        (1, lambda i: sum_pass(0, i)),
        (2, after_self),
        (3, lambda i: gather_pass(r.buf_a, i)),
        (4, feed),
        (4, lambda i: at(i, n - 1, feed_grads)),
        (5, lambda i: sum_pass(0, i)),
        (6, after_feed),
        (7, lambda i: gather_pass(r.buf_b2, i)),
        (8, self_back),
        (8, lambda i: sum_pass(1, i)),
    )

    r.grad_up[:, C : 2 * C] = r.grad_key[:, : z.tokens].T.astype(bf16)
    r.grad_up[:, 2 * C : 3 * C] = r.grad_value[:, : z.tokens].T.astype(bf16)

    clear_keys()

    def self_down(i):
        sum_start(0, i, nt(r.grad_up[chunk(i), : 3 * C], W[QKV][...].reshape(D, 3 * C)))

        @functools.partial(at, i, 0)
        def _():
            value = tn(r.att2[...], r.buf_b2[...].reshape(z.tokens, D)).astype(bf16)
            r.grads_c[1] = value.reshape(2, z.block, D)

        @functools.partial(at, i, n - 1)
        def _():
            grads_into(r.grads_b, whole(r.buf_h2), lambda: r.grad_up[:, : 3 * C], 3 * C)

    def after_self_down(i):
        grad, shift, scale = norm_backward(r.x1[i], mod(3), sum_end(0, i))
        keep_sums(2, shift, scale)
        grad = r.dx[i] + grad
        r.dx[i] = grad
        r.buf_b[i, s] = grad.astype(bf16)
        gather_start(r.buf_b, i)

    def cross_back(i):
        gather_wait(r.buf_b, i)
        grad = nt(r.buf_b[i].reshape(rows, D), W[OC][...].reshape(C, D)).astype(bf16)

        @functools.partial(at, i, n - 1)
        def _():
            value = tn(r.att1[...], r.buf_b[...].reshape(z.tokens, D)).astype(bf16)
            r.grads_c[0] = value.reshape(2, z.block, D)
            grad_start(11)

        attend_back(i, *cross, grad, mask_rows, r.hidden)
        sum_start(0, i, nt(r.hidden[chunk(i), :C], W[Q][...].reshape(D, C)))

    def after_cross_back(i):
        grad, shift, scale = norm_backward(r.x0[i].astype(f32), mod(1), sum_end(0, i))
        keep_sums(0, shift, scale)
        r.dx[i] += grad

    def last_grads():
        grads_into(r.grads_a, lambda lane: r.normed1[:, lane], lambda: r.hidden[:, :C], C)
        grad_start(12)
        for side, rest in enumerate((r.grad_key[...], r.grad_value[...])):
            total = None
            for _ in range(3):
                term = rest.astype(bf16)
                rest = rest - term.astype(f32)
                product_term = nn(term[:, : z.whole_rows], r.image_all[: z.whole_rows, :])
                product_term = product_term + nn(term[:, z.whole_rows :], r.tail[...])
                total = product_term if total is None else total + product_term
            value = total.T.astype(bf16)
            for o in range(B):
                r.grads_a[o // 2, o % 2, : z.image_block, C + side * C : C + (side + 1) * C] = value[
                    o * z.image_block : (o + 1) * z.image_block
                ]
        grad_start(13)

    pipeline(
        {
            0: [(grad_pass, 3), (grad_start, 6), (grad_end, 0)],
            1: [(grad_pass, 4), (grad_start, 7), (grad_end, 1)],
            3: [(grad_pass, 5), (grad_start, 8)],
            4: [(grad_pass, 6), (grad_end, 2), (grad_start, 9)],
            5: [(grad_pass, 7), (grad_end, 3), (grad_start, 10)],
            6: [(grad_pass, 8), (grad_end, 4), (grad_end, 5)],
            7: [(grad_turn, 8), (grad_pass, 9), (grad_end, 6), (grad_relay, 0), (grad_relay, 1)],
            8: [(grad_pass, 10), (grad_end, 7), (grad_relay, 2), (grad_relay, 3)],
            9: [(grad_end, 8), (grad_end, 9), (grad_relay, 4), (grad_relay, 5)],
        },
        (0, self_down),
        (1, lambda i: sum_pass(0, i)),
        (2, after_self_down),
        (3, lambda i: gather_pass(r.buf_b, i)),
        (3, layer_output),
        (4, cross_back),
        (4, lambda i: at(i, n - 1, last_grads)),
        (5, lambda i: sum_pass(0, i)),
        (6, after_cross_back),
    )
    grad_copy = pltpu.make_async_copy(r.dx, r.grad_tokens, r.sem_out.at[0])
    grad_copy.start()

    def sums_send(j):
        return remote(
            r.sums, r.sums_seq.at[s], r.sem_d_s.at[j - 1], r.sem_d_r.at[s], (b, lax.rem(s + j, S))
        )

    for j in range(1, S):
        sums_send(j).start()
    run([(grad_pass, 11), (grad_end, 10)])
    total = r.sums[...]
    for j in range(1, S):
        k = lax.rem(s + j, S)
        arrived(r.sums_seq.at[k], r.sem_d_s.at[0], r.sem_d_r.at[k], (b, k))
        total = total + r.sums_seq[k]
    r.mods_all[b] = total

    def table_send(j):
        return remote(
            r.mods_all.at[b],
            r.mods_all.at[b],
            r.sem_t_s.at[j - 1],
            r.sem_t_r.at[b],
            (lax.rem(b + j, B), s),
        )

    for j in range(1, B):
        table_send(j).start()
    run([(grad_pass, 12), (grad_turn, 11), (grad_pass, 13)])
    for j in range(1, B):
        k = lax.rem(b + j, B)
        arrived(r.mods_all.at[k], r.sem_t_s.at[0], r.sem_t_r.at[k], (k, s))
    table_copy = pltpu.make_async_copy(r.mods_all, r.table, r.sem_out.at[1])
    table_copy.start()
    run([(grad_end, 11), (grad_end, 12), (grad_end, 13)])
    run([(grad_relay, k) for k in range(6, len(SCATTER))])
    for j in range(1, S):
        sums_send(j).wait_send()
    for j in range(1, B):
        table_send(j).wait_send()
    for k in range(len(GATHER)):
        weight_drain(k)
    for k in range(len(SCATTER)):
        grad_drain(k)
    for i in range(n):
        output_copy(i).wait()
    grad_copy.wait()
    table_copy.wait()


def layer_call(z, args):
    n, part, D, C, S, B = z.chunks, z.part, z.width, z.columns, z.seq, z.batch
    Z = B // 2
    own = (n, part, D)
    full = (n, S, part, D)
    vmem = pltpu.VMEM
    dma = pltpu.SemaphoreType.DMA
    weights = [
        vmem((2, z.block, D) if w in BY_ROWS else (B,) + shape, bf16)
        for w, shape in enumerate(z.weights)
    ]
    firsts = [
        vmem((z.block, D) if w in BY_ROWS else (Z,) + shape, bf16)
        for w, shape in enumerate(z.weights)
    ]
    seconds = [vmem((Z - 1,) + shape, bf16) for shape in z.weights]
    lane = [
        vmem((n, 2, 2, part, D), bf16),
        vmem((n, 2, part, D), bf16),
        vmem((n, part, D), bf16),
        vmem((n, part, D), bf16),
    ]
    scratch = (
        weights
        + firsts
        + seconds
        + [vmem(full, bf16)] * 4
        + lane
        + lane
        + [
            vmem((Z,) + z.weights[OC], bf16),
            vmem((Z,) + z.weights[OS], bf16),
            vmem((S,) + z.weights[OC], bf16),
            vmem((S,) + z.weights[OS], bf16),
            vmem((z.image_rows, z.image_width), bf16),
            vmem((z.keys - z.whole_rows, z.image_width), bf16),
            vmem((1, z.image_rows), jnp.int32),
            vmem((8, z.keys), f32),
            vmem(args[5].shape, bf16),
            vmem((B, 8, D), f32),
            vmem((8, D), f32),
            vmem((8, D), f32),
            vmem((S, 8, D), f32),
            vmem((z.tokens, D), bf16),
            vmem((z.tokens, C), bf16),
            vmem((z.keys, C), bf16),
            vmem((z.keys, C), bf16),
            vmem((z.tokens, C), bf16),
            vmem((z.tokens, 3 * C), bf16),
            vmem((z.tokens, C), bf16),
            vmem((z.tokens, z.hidden), bf16),
            vmem((z.tokens, z.hidden), bf16),
            vmem((C, z.keys), f32),
            vmem((C, z.keys), f32),
            vmem(own, bf16),
            vmem(own, f32),
            vmem(own, f32),
            vmem(own, f32),
            vmem((Z, 2, z.block, D), bf16),
            vmem((Z, 2, z.block, D), bf16),
            vmem((2, 2, z.block, D), bf16),
            dma((33,)),
            dma((len(GATHER), Z)),
            dma((len(GATHER), Z)),
            dma((len(GATHER), Z)),
            dma((len(GATHER), Z)),
            dma((len(SCATTER),)),
            dma((len(SCATTER),)),
            dma((len(SCATTER), 3)),
            dma((len(SCATTER), Z)),
            dma((len(SCATTER), 3)),
            dma((len(SCATTER), 3)),
            dma((len(SCATTER),)),
            dma((2, S - 1)),
            dma((2, S)),
            dma((2, S - 1)),
            dma((2, S)),
            dma((2, 3)),
            dma((2, 3)),
            dma((n, 3)),
            dma((n, 3)),
            dma((2, n, 2)),
            dma((2, n, 2)),
            dma((B - 1,)),
            dma((B,)),
            dma((S - 1,)),
            dma((S,)),
            dma((B - 1,)),
            dma((B,)),
            dma((2 + n,)),
        ]
    )
    shape = jax.ShapeDtypeStruct
    outs = [shape(own, bf16), shape(own, f32), shape((B, 8, D), f32)] + [
        shape((S,) + size, bf16) for size in z.weights
    ]
    anywhere = pl.BlockSpec(memory_space=pl.ANY)
    scalars = pl.BlockSpec(memory_space=pltpu.SMEM)
    return pl.pallas_call(
        functools.partial(whole_layer, z),
        out_shape=outs,
        in_specs=[anywhere] * 4 + [scalars] + [anywhere] * (len(args) - 5),
        out_specs=[anywhere] * len(outs),
        scratch_shapes=scratch,
        compiler_params=pltpu.CompilerParams(
            collective_id=0, has_side_effects=True, vmem_limit_bytes=LIMIT
        ),
        name="whole_layer",
    )(*args)


def finish(z, camera, output, grad_tokens, table, *refs):
    grads, outs = refs[:7], refs[7:]
    gate_t = refs[-1]
    step = pl.program_id(0)
    outs[0][...] = output[...]
    outs[1][...] = grad_tokens[...]

    @pl.when(step == 0)
    def _():
        own = camera[...].astype(f32)
        gate_t[...] = (own * jax.nn.sigmoid(own)).astype(bf16).astype(f32).T

    lanes = z.block // z.seq
    gate = gate_t[pl.ds(pl.multiple_of(step * lanes, 8), lanes), :]
    for k in range(6):
        outs[2][:, k * z.width : (k + 1) * z.width] = jnp.dot(
            gate, table[:, k, :], precision=highest, preferred_element_type=f32
        )

    def across(w, out, groups):
        width = grads[w].shape[2] // groups
        for j in range(z.seq):
            for g in range(groups):
                column = (g * z.seq + j) * width
                out[:, column : column + width] = grads[w][j, :, g * width : (g + 1) * width].astype(f32)

    across(Q, outs[3], 1)
    across(KV, outs[4], 2)
    outs[5][...] = grads[OC][0].astype(f32)
    across(QKV, outs[6], 3)
    outs[7][...] = grads[OS][0].astype(f32)
    across(UP, outs[8], z.batch)
    outs[9][...] = grads[DOWN][0].astype(f32)


def finish_call(z, camera, output, grad_tokens, table, *grads):
    S, D = z.seq, z.width
    n = z.chunks // S
    few = z.block // S
    few_image = z.image_block // S
    own = pl.BlockSpec((n, z.part, D), lambda i: (i, 0, 0))
    whole = pl.BlockSpec(table.shape, lambda i: (0, 0, 0))

    def quarter(w):
        if w in (OC, OS, DOWN):
            return pl.BlockSpec((1,) + grads[w].shape[1:], lambda i: (i, 0, 0))
        return pl.BlockSpec((S, grads[w].shape[1] // S, grads[w].shape[2]), lambda i: (0, i, 0))

    def rows(count, width):
        return pl.BlockSpec((count, width), lambda i: (i, 0))

    sizes = (
        (few, z.block, 6 * D),
        (few, z.block, D),
        (few_image, z.image_block, 2 * D),
        (few, z.block, D),
        (few, z.block, 3 * D),
        (few, z.block, D),
        (few, z.block, S * z.hidden),
        (z.hidden // z.batch, S * z.hidden // z.batch, D),
    )
    results = pl.pallas_call(
        functools.partial(finish, z),
        grid=(S,),
        out_shape=[
            jax.ShapeDtypeStruct(output.shape, bf16),
            jax.ShapeDtypeStruct(grad_tokens.shape, f32),
        ]
        + [jax.ShapeDtypeStruct((count, width), f32) for _, count, width in sizes],
        in_specs=[pl.BlockSpec(camera.shape, lambda i: (0, 0)), own, own, whole]
        + [quarter(w) for w in range(7)],
        out_specs=[own, own] + [rows(block, width) for block, _, width in sizes],
        scratch_shapes=[pltpu.VMEM((camera.shape[1], camera.shape[0]), f32)],
        compiler_params=pltpu.CompilerParams(vmem_limit_bytes=LIMIT),
        name="finish",
    )(camera, output, grad_tokens, table, *grads)
    output, grad_tokens, *rest = results
    return (output.reshape(1, z.own, D), grad_tokens.reshape(1, z.own, D), *rest)


def local_kernel(sizes, *inputs):
    (
        tokens,
        cotangent,
        image_tokens,
        image_lengths,
        key_mask,
        camera,
        modulation,
        q_cross,
        kv_image,
        out_cross,
        qkv_self,
        out_self,
        mlp_in,
        mlp_out,
    ) = inputs
    z = sizes
    n, part, D, C, S, B = z.chunks, z.part, z.width, z.columns, z.seq, z.batch
    results = layer_call(
        z,
        (
            tokens[0].reshape(n, part, D),
            cotangent[0].reshape(n, part, D),
            image_tokens[0],
            key_mask,
            image_lengths,
            camera,
            modulation,
            q_cross,
            kv_image,
            out_cross,
            qkv_self,
            out_self,
            mlp_in,
            mlp_out,
        ),
    )
    return finish_call(z, camera, *results)


def fits(mesh, inputs):
    batch, seq = mesh.shape["batch"], mesh.shape["seq"]
    own, width = inputs[0].shape[1:]
    return (
        batch == 8
        and seq == 4
        and own % 64 == 0
        and width == HEADS * HEAD_DIM
        and (width // seq) % 128 == 0
        and (inputs[12].shape[1] // seq // batch) % 128 == 0
    )


def choose(mesh, *inputs):
    if not fits(mesh, inputs):
        return local(*inputs)
    return local_kernel(Sizes(mesh.shape, inputs), *inputs)


def solution(mesh):
    return jax.shard_map(
        functools.partial(choose, mesh),
        mesh=mesh,
        in_specs=(
            P("batch", "seq", None),
            P("batch", "seq", None),
            P("batch", None, None),
            P("batch"),
            P("batch", None),
            P(None, "batch"),
            P("batch", None),
            P("batch", None),
            P("batch", None),
            P("batch", None),
            P("batch", None),
            P("batch", None),
            P("batch", None),
            P("batch", None),
        ),
        out_specs=(
            P("batch", "seq", None),
            P("batch", "seq", None),
            P("batch", None),
            P("batch", None),
            P("batch", None),
            P("batch", None),
            P("batch", None),
            P("batch", None),
            P("batch", None),
            P("batch", None),
        ),
        check_vma=False,
    )
```

profile of v0, /device:TPU:17, one launch (start us, length us, event | category | flops | bytes accessed | tf_op | source)
XLA Modules:
  0.0 273.1 jit_solution(15952830788423859533)
XLA Ops:
  1.3 263.0 %whole_layer.1 = (bf16[4,64,1024]{2,1,0:T(8,128)(2,1)}, f32[4,64,1024]{2,1,0:T(8,128)}, f32[8,8,1024]{2,1,0:T(8,128)}, bf16[4,128,256]{2,1,0:T(8,128)(2,1)}, bf1...) custom-call(bf16[4,64,1024]{2,1,0:T(8,128)(2,1)} %bitcast.6, ...), custom_call_target="tpu_custom_call" | custom-call | tf_op jit(solution)/shard_map/whole_layer/pallas_call | solution.py:1512
  264.3 8.6 %finish.1 = (bf16[4,64,1024]{2,1,0:T(8,128)(2,1)}, f32[4,64,1024]{2,1,0:T(8,128)}, f32[128,6144]{1,0:T(8,128)}, f32[128,1024]{1,0:T(8,128)}, f32[96,2048]{1,0:T(...) custom-call(bf16[8,128]{1,0:T(8,128)(2,1)} %camera.1, ...), custom_call_target="tpu_custom_call" | custom-call | tf_op jit(solution)/shard_map/finish/pallas_call | solution.py:1586
where the time goes:
time: 276 us; the launch traced here: 273 us
  Pallas kernels  272 us (99%)
    pallas_call x1, Pallas kernels, layer_call(): pl.pallas_call(functools.partial(whole_layer, z), out_shape=outs, in_spec...  263 us
    pallas_call x1, Pallas kernels, finish_call(): pl.pallas_call(functools.partial(finish, z), grid=(S,), out_shape=[jax.Sh...  8.61 us

commit v1 on v0

--- a/solution.py
+++ b/solution.py
@@ -402,11 +402,15 @@
     (QKV, 0, 2),
     (QKV, 1, 2),
     (OC, 0, 1),
-    (Q, 0, 1),
-    (KV, 0, 1),
+    (Q, 0, 2),
+    (Q, 1, 2),
+    (KV, 0, 3),
+    (KV, 1, 3),
+    (KV, 2, 3),
 )
 BY_ROWS = (OC, OS)
 AHEAD = 2
+EARLY = (3, 4, 6, 7, 8, 9)
 
 
 class Sizes:
@@ -681,12 +685,12 @@
         if k >= len(GATHER):
             return
         w, which, _ = GATHER[k]
-        if which == 0:
+        if which == 0 and k not in EARLY:
             loaded(w)
         z_send(k, 2).start()
         for j in (1, 3):
             pl.when(z_near(j))(z_send(k, j).start)
-        if w not in BY_ROWS:
+        if w not in BY_ROWS and k not in EARLY:
             x_send(k, zz).start()
 
     def weight_came(k, j):
@@ -980,6 +984,10 @@
             r.x2[0, 8 * o + k : 8 * o + k + 1, :] = term[o : o + 1, :]
     for j in range(1, B):
         mods_send(j).start()
+    for k in EARLY:
+        if GATHER[k][1] == 0:
+            loaded(GATHER[k][0])
+        x_send(k, zz).start()
     loaded(COTANGENT)
     input_start(r.buf_b, 1)
     loaded(IMAGE)
@@ -1321,8 +1329,10 @@
         r.dx[i] += grad
 
     def last_grads():
+        grad_pass(11)
         grads_into(r.grads_a, lambda lane: r.normed1[:, lane], lambda: r.hidden[:, :C], C)
         grad_start(12)
+        grad_start(13)
         for side, rest in enumerate((r.grad_key[...], r.grad_value[...])):
             total = None
             for _ in range(3):
@@ -1336,19 +1346,21 @@
                 r.grads_a[o // 2, o % 2, : z.image_block, C + side * C : C + (side + 1) * C] = value[
                     o * z.image_block : (o + 1) * z.image_block
                 ]
-        grad_start(13)
+        grad_start(14)
+        grad_start(15)
 
     pipeline(
         {
             0: [(grad_pass, 3), (grad_start, 6), (grad_end, 0)],
             1: [(grad_pass, 4), (grad_start, 7), (grad_end, 1)],
+            2: [(weight_drain, k) for k in range(len(GATHER))],
             3: [(grad_pass, 5), (grad_start, 8)],
             4: [(grad_pass, 6), (grad_end, 2), (grad_start, 9)],
             5: [(grad_pass, 7), (grad_end, 3), (grad_start, 10)],
             6: [(grad_pass, 8), (grad_end, 4), (grad_end, 5)],
             7: [(grad_turn, 8), (grad_pass, 9), (grad_end, 6), (grad_relay, 0), (grad_relay, 1)],
-            8: [(grad_pass, 10), (grad_end, 7), (grad_relay, 2), (grad_relay, 3)],
-            9: [(grad_end, 8), (grad_end, 9), (grad_relay, 4), (grad_relay, 5)],
+            8: [(grad_pass, 10), (grad_turn, 11), (grad_end, 7), (grad_relay, 2), (grad_relay, 3)],
+            9: [(grad_pass, 12), (grad_pass, 13), (grad_end, 8), (grad_end, 9), (grad_relay, 4), (grad_relay, 5)],
         },
         (0, self_down),
         (1, lambda i: sum_pass(0, i)),
@@ -1370,7 +1382,7 @@
 
     for j in range(1, S):
         sums_send(j).start()
-    run([(grad_pass, 11), (grad_end, 10)])
+    run([(grad_pass, 14), (grad_start, 16), (grad_end, 10)])
     total = r.sums[...]
     for j in range(1, S):
         k = lax.rem(s + j, S)
@@ -1389,21 +1401,20 @@
 
     for j in range(1, B):
         table_send(j).start()
-    run([(grad_pass, 12), (grad_turn, 11), (grad_pass, 13)])
+    run([(grad_pass, 15), (grad_end, 11), (grad_end, 12), (grad_pass, 16), (grad_end, 13)])
     for j in range(1, B):
         k = lax.rem(b + j, B)
         arrived(r.mods_all.at[k], r.sem_t_s.at[0], r.sem_t_r.at[k], (k, s))
     table_copy = pltpu.make_async_copy(r.mods_all, r.table, r.sem_out.at[1])
     table_copy.start()
-    run([(grad_end, 11), (grad_end, 12), (grad_end, 13)])
+    run([(grad_end, 14), (grad_end, 15), (grad_end, 16)])
     run([(grad_relay, k) for k in range(6, len(SCATTER))])
+    run([(grad_drain, k) for k in range(6)])
     for j in range(1, S):
         sums_send(j).wait_send()
     for j in range(1, B):
         table_send(j).wait_send()
-    for k in range(len(GATHER)):
-        weight_drain(k)
-    for k in range(len(SCATTER)):
+    for k in range(6, len(SCATTER)):
         grad_drain(k)
     for i in range(n):
         output_copy(i).wait()

time: 276 us -> 273 us (0.989)
  no operation moved by 1% of the time
where the time goes in v1:
time: 273 us; the launch traced here: 271 us
  Pallas kernels  270 us (99%)
    pallas_call x1, Pallas kernels, layer_call(): pl.pallas_call(functools.partial(whole_layer, z), out_shape=outs, in_spec...  261 us
    pallas_call x1, Pallas kernels, finish_call(): pl.pallas_call(functools.partial(finish, z), grid=(S,), out_shape=[jax.Sh...  8.61 us

profile of v1, /device:TPU:17, one launch (start us, length us, event | category | flops | bytes accessed | tf_op | source)
XLA Modules:
  0.0 271.4 jit_solution(13893795711144251939)
XLA Ops:
  1.3 261.3 %whole_layer.1 = (bf16[4,64,1024]{2,1,0:T(8,128)(2,1)}, f32[4,64,1024]{2,1,0:T(8,128)}, f32[8,8,1024]{2,1,0:T(8,128)}, bf16[4,128,256]{2,1,0:T(8,128)(2,1)}, bf1...) custom-call(bf16[4,64,1024]{2,1,0:T(8,128)(2,1)} %bitcast.6, ...), custom_call_target="tpu_custom_call" | custom-call | tf_op jit(solution)/shard_map/whole_layer/pallas_call | solution.py:1523
  262.6 8.6 %finish.1 = (bf16[4,64,1024]{2,1,0:T(8,128)(2,1)}, f32[4,64,1024]{2,1,0:T(8,128)}, f32[128,6144]{1,0:T(8,128)}, f32[128,1024]{1,0:T(8,128)}, f32[96,2048]{1,0:T(...) custom-call(bf16[8,128]{1,0:T(8,128)(2,1)} %camera.1, ...), custom_call_target="tpu_custom_call" | custom-call | tf_op jit(solution)/shard_map/finish/pallas_call | solution.py:1597
